TPU v7x, 32 devices: a whole 2x2x4 slice. The times are simulated.
32 devices in a mesh: dp: 4 (over y, x), seq: 4 (over z), tp: 2 (over core).
Axes of the slice: x: 2, y: 2, z: 4, core: 2. Of those that a mesh axis runs over, the one named last changes fastest.
Arguments:
- queries: bfloat16 [4, 2048, 5120], P('dp', 'seq', 'tp'), may hold values from -200 to 200
- keys: bfloat16 [4, 512, 5120], P('dp', None, 'tp'), may hold values from -6 to 6
- values: bfloat16 [4, 512, 5120], P('dp', None, 'tp'), may hold values from -6 to 6
- grad_attention: bfloat16 [4, 2048, 5120], P('dp', 'seq', 'tp'), may hold values from -48 to 48
- normed: bfloat16 [4, 512, 4096], P('dp', None, 'seq'), may hold values from -6 to 6
- norm_scale: float32 [4, 512], P('dp'), may hold values from 0.3 to 3
- norm_gain: float32 [4096], P('seq'), may hold values from 0.1 to 1.9
- key_weight: bfloat16 [4096, 5120], P('seq', 'tp'), may hold values from -0.078125 to 0.078125
- value_weight: bfloat16 [4096, 5120], P('seq', 'tp'), may hold values from -0.078125 to 0.078125
- key_down: bfloat16 [4096, 32], P('seq'), may hold values from -0.09375 to 0.09375
- key_up: bfloat16 [32, 5120], P(None, 'tp'), may hold values from -0.078125 to 0.078125
- value_down: bfloat16 [4096, 32], P('seq'), may hold values from -0.09375 to 0.09375
- value_up: bfloat16 [32, 5120], P(None, 'tp'), may hold values from -0.078125 to 0.078125
- out_weight: bfloat16 [10240, 4096], P('tp', 'seq'), may hold values from -0.09375 to 0.09375
Outputs:
- grad_queries: bfloat16 [4, 2048, 5120], P('dp', 'seq', 'tp')
- grad_text: bfloat16 [4, 512, 4096], P('dp', None, 'seq')
- grad_hidden: bfloat16 [4, 512, 10240], P('dp', 'seq', 'tp')
- grad_key_down: float32 [4096, 32], P('seq')
- grad_key_up: float32 [32, 5120], P(None, 'tp')
- grad_value_down: float32 [4096, 32], P('seq')
- grad_value_up: float32 [32, 5120], P(None, 'tp')
All inputs are finite; a program needn't handle non-finite values.
Results may differ from a plain program's by a relative error of at most 0.03.
Values may be sent and summed in bfloat16 or wider, within the bound.
A program may use at most 192 MiB of HBM per device.

v0:
```python
import jax
import jax.numpy as jnp
from jax import lax
from jax.sharding import PartitionSpec as P

HD = 128
DT = 4096


def contract_last(left_side, right_side):
    return lax.dot_general(
        left_side, right_side, (((1,), (1,)), ((), ())), preferred_element_type=jnp.float32
    )


def contract_first(left_side, right_side):
    return lax.dot_general(
        left_side, right_side, (((0,), (0,)), ((), ())), preferred_element_type=jnp.float32
    )


def attention_grads(queries, keys, values, grad_attention):
    row_count, columns = queries.shape
    length = keys.shape[0]
    head_count = columns // HD
    factor = HD ** (-0.5)
    query_heads = queries.reshape(row_count, head_count, HD)
    key_heads = keys.reshape(length, head_count, HD)
    value_heads = values.reshape(length, head_count, HD)
    grad_heads = grad_attention.reshape(row_count, head_count, HD)
    scores = (
        jnp.einsum("ihd,jhd->hij", query_heads, key_heads, preferred_element_type=jnp.float32)
        * factor
    )
    weights = jnp.exp(scores - jnp.max(scores, axis=2, keepdims=True))
    probability = weights / jnp.sum(weights, axis=2, keepdims=True)
    weights_low = probability.astype(jnp.bfloat16)
    grad_probs = jnp.einsum(
        "ihd,jhd->hij", grad_heads, value_heads, preferred_element_type=jnp.float32
    )
    grad_scores = probability * (
        grad_probs - jnp.sum(probability * grad_probs, axis=2, keepdims=True)
    )
    grad_low = grad_scores.astype(jnp.bfloat16)
    grad_query = (
        jnp.einsum("hij,jhd->ihd", grad_low, key_heads, preferred_element_type=jnp.float32) * factor
    )
    grad_key = (
        jnp.einsum("hij,ihd->jhd", grad_low, query_heads, preferred_element_type=jnp.float32)
        * factor
    )
    grad_value = jnp.einsum(
        "hij,ihd->jhd", weights_low, grad_heads, preferred_element_type=jnp.float32
    )
    return (
        grad_query.astype(jnp.bfloat16).reshape(row_count, columns),
        grad_key.reshape(length, columns),
        grad_value.reshape(length, columns),
    )


def norm_backward(
    context_base, key_back, value_back, text_rows, scale_rows, norm_gain, key_down, value_down
):
    grad_context = (
        context_base + contract_last(key_back, key_down) + contract_last(value_back, value_down)
    )
    text_values = text_rows.astype(jnp.float32)
    scaled = norm_gain * grad_context
    local_sum = jnp.sum(text_values * scaled, axis=1)
    token_sum = lax.psum(local_sum, "seq")
    return (scale_rows[:, None] * (scaled - text_values * (token_sum / DT)[:, None])).astype(
        jnp.bfloat16
    )


def shards(
    queries,
    keys,
    values,
    grad_attention,
    normed,
    norm_scale,
    norm_gain,
    key_weight,
    value_weight,
    key_down,
    key_up,
    value_down,
    value_up,
    out_weight,
):
    grad_query, grad_key, grad_value = attention_grads(
        queries[0], keys[0], values[0], grad_attention[0]
    )
    context = (normed[0].astype(jnp.float32) * norm_gain).astype(jnp.bfloat16)
    key_part = jnp.dot(context, key_down, preferred_element_type=jnp.float32)
    value_part = jnp.dot(context, value_down, preferred_element_type=jnp.float32)
    key_sum, value_sum, key_lowsum, value_lowsum = (
        lax.psum(grad_key.astype(jnp.bfloat16), "seq").astype(jnp.float32),
        lax.psum(grad_value.astype(jnp.bfloat16), "seq").astype(jnp.float32),
        lax.psum(key_part.astype(jnp.bfloat16), "seq").astype(jnp.float32),
        lax.psum(value_part.astype(jnp.bfloat16), "seq").astype(jnp.float32),
    )
    key_grad = key_sum.astype(jnp.bfloat16)
    value_grad = value_sum.astype(jnp.bfloat16)
    key_latent = key_lowsum.astype(jnp.bfloat16)
    value_latent = value_lowsum.astype(jnp.bfloat16)
    key_project = contract_last(key_grad, key_up)
    value_project = contract_last(value_grad, value_up)
    context_part = contract_last(key_grad, key_weight) + contract_last(value_grad, value_weight)
    context_base, key_total, value_total = (
        lax.psum(context_part.astype(jnp.bfloat16), "tp").astype(jnp.float32),
        lax.psum(key_project.astype(jnp.bfloat16), "tp").astype(jnp.float32),
        lax.psum(value_project.astype(jnp.bfloat16), "tp").astype(jnp.float32),
    )
    key_back = key_total.astype(jnp.bfloat16)
    value_back = value_total.astype(jnp.bfloat16)
    grad_text = norm_backward(
        context_base,
        key_back,
        value_back,
        normed[0],
        norm_scale[0],
        norm_gain,
        key_down,
        value_down,
    )
    prompt_count = lax.axis_size("dp")
    down_key = contract_first(context, key_back)
    down_value = contract_first(context, value_back)
    up_key = contract_first(key_latent, key_grad)
    up_value = contract_first(value_latent, value_grad)
    down_key, up_key, down_value, up_value = (
        lax.psum(down_key.astype(jnp.bfloat16), "dp").astype(jnp.float32),
        lax.psum(up_key.astype(jnp.bfloat16), "dp").astype(jnp.float32),
        lax.psum(down_value.astype(jnp.bfloat16), "dp").astype(jnp.float32),
        lax.psum(up_value.astype(jnp.bfloat16), "dp").astype(jnp.float32),
    )
    grad_hidden = lax.psum_scatter(
        contract_last(grad_text, out_weight).astype(jnp.bfloat16),
        "seq",
        scatter_dimension=0,
        tiled=True,
    )
    return (
        grad_query[None],
        grad_text[None],
        grad_hidden[None],
        down_key / prompt_count,
        up_key / prompt_count,
        down_value / prompt_count,
        up_value / prompt_count,
    )


def solution(mesh):
    return jax.shard_map(
        shards,
        mesh=mesh,
        in_specs=(
            P("dp", "seq", "tp"),
            P("dp", None, "tp"),
            P("dp", None, "tp"),
            P("dp", "seq", "tp"),
            P("dp", None, "seq"),
            P("dp", None),
            P("seq"),
            P("seq", "tp"),
            P("seq", "tp"),
            P("seq", None),
            P(None, "tp"),
            P("seq", None),
            P(None, "tp"),
            P("tp", "seq"),
        ),
        out_specs=(
            P("dp", "seq", "tp"),
            P("dp", None, "seq"),
            P("dp", "seq", "tp"),
            P("seq", None),
            P(None, "tp"),
            P("seq", None),
            P(None, "tp"),
        ),
        check_vma=False,
    )
```

profile of v0, /device:TPU:0, one launch (start us, length us, event | category | flops | bytes accessed | tf_op | source)
XLA Modules:
  0.0 517.3 jit_solution(190219239213551095)
XLA Ops:
  7.2 4.4 copy.32
  14.6 4.4 copy.36
  19.0 4.4 copy.37
  23.4 12.1 %fusion.22 = (f32[20,512]{1,0:T(8,128)S(1)}, f32[20,512,512]{1,2,0:T(8,128)}) fusion(bf16[512,20,128]{0,2,1:T(8,128)(2,1)} %bitcast.63, bf16[512,20,128]{0,2,1:T(8,128)(2,1)S(1)} %bitcast.58), kind=kOutput, calls=%fused_computation.39 | convolution fusion | flops 1357906432 | bytes 26255360 | tf_op jit(solution)/shard_map/sub | solution.py:35
  35.5 10.9 %fusion.14 = bf16[20,512,128]{1,2,0:T(8,128)(2,1)} fusion(bf16[512,20,128]{0,2,1:T(8,128)(2,1)} %bitcast.65, f32[20,512,512]{1,2,0:T(8,128)} %get-tuple-element.32, f32[20,512]{1,0:T(8,128)S(1)} %get-tuple-element.31), kind=kOutput, calls=%fused_computation.26 | convolution fusion | flops 1353973760 | bytes 26255360 | tf_op jit(solution)/shard_map/hij,ihd->jhd/dot_general | solution.py:52
  46.5 15.6 %multiply_reduce_fusion = (f32[20,512]{1,0:T(8,128)S(1)}, f32[20,512,512]{1,2,0:T(8,128)}) fusion(f32[20,512,512]{1,2,0:T(8,128)} %get-tuple-element.32, f32[20,512]{1,0:T(8,128)S(1)} %get-tuple-element.31, bf16[512,20,128]{0,2,1:T(8,128)(2,1)} %bitcast.66, bf16[512,20,128]{0,2,1:T(8,128)(2,1)} %bitcast.67), kind=kOutput, calls=%fused_computation.2 | convolution fusion | flops 1357895680 | bytes 47267840 | tf_op jit(solution)/shard_map/ihd,jhd->hij/dot_general | solution.py:38
  62.1 18.7 %multiply_convert_fusion = bf16[20,512,512]{1,2,0:T(8,128)(2,1)} fusion(f32[20,512,512]{1,2,0:T(8,128)} %get-tuple-element.34, f32[20,512]{1,0:T(8,128)S(1)} %get-tuple-element.33, f32[20,512,512]{1,2,0:T(8,128)} %get-tuple-element.32, f32[20,512]{1,0:T(8,128)S(1)} %get-tuple-element.31), kind=kLoop, calls=%fused_computation.1 | loop fusion | flops 20971520 | bytes 52510720 | tf_op jit(solution)/shard_map/convert_element_type | solution.py:44
  80.8 9.7 %multiply_convert_fusion.1 = bf16[20,512,128]{1,2,0:T(8,128)(2,1)} fusion(bf16[20,512,512]{1,2,0:T(8,128)(2,1)} %multiply_convert_fusion, bf16[512,20,128]{0,2,1:T(8,128)(2,1)} %bitcast.64), kind=kOutput, calls=%fused_computation.11 | convolution fusion | flops 1344798720 | bytes 15728640 | tf_op jit(solution)/shard_map/hij,ihd->jhd/dot_general | solution.py:49
  96.2 186.2 %all-reduce.14.cloned.1.call-done = (bf16[512,2560]{0,1:T(8,128)(2,1)}, bf16[512,2560]{0,1:T(8,128)(2,1)}) async-done(((bf16[512,2560]{0,1:T(8,128)(2,1)}, bf16[512,2560]{0,1:T(8,128)(2,1)}), (bf16[512,2560]{0,1:T(8,128)(2,1)}, bf16[512,2560]{0,1:T(8,128)(2,1)})) %all-reduce.14.cloned.1.call-update) | async-done | bytes 5242896 | tf_op jit(solution)/shard_map/psum | solution.py:100
  282.4 3.1 convolution_convert_fusion.7
  285.5 5.1 fusion.23
  290.6 6.4 %add_convert_fusion = bf16[512,1024]{1,0:T(8,128)(2,1)} fusion(f32[512,1024]{1,0:T(8,128)S(1)} %fusion.23, bf16[512,2560]{0,1:T(8,128)(2,1)S(1)} %copy-done.2, bf16[1024,2560]{1,0:T(8,128)(2,1)} %param.22), kind=kOutput, calls=%fused_computation.25 | convolution fusion | flops 2685403136 | bytes 11010048 | tf_op jit(solution)/shard_map/dot_general | solution.py:11
  300.0 20.0 %all-reduce.12.cloned.1.call-done = (bf16[512,32]{1,0:T(8,128)(2,1)}, bf16[512,32]{1,0:T(8,128)(2,1)}) async-done(((bf16[512,32]{1,0:T(8,128)(2,1)}, bf16[512,32]{1,0:T(8,128)(2,1)}), (bf16[512,32]{1,0:T(8,128)(2,1)}, bf16[512,32]{1,0:T(8,128)(2,1)})) %all-reduce.12.cloned.1.call-update) | async-done | bytes 65552 | tf_op jit(solution)/shard_map/psum | solution.py:102
  320.0 3.4 convolution_convert_fusion.1
  323.5 3.3 convolution_convert_fusion.2
  326.8 13.7 %all-reduce.18.cloned.1.call-done = (bf16[512,32]{0,1:T(8,128)(2,1)}, bf16[512,32]{0,1:T(8,128)(2,1)}) async-done(((bf16[512,32]{0,1:T(8,128)(2,1)}, bf16[512,32]{0,1:T(8,128)(2,1)}), (bf16[512,32]{0,1:T(8,128)(2,1)}, bf16[512,32]{0,1:T(8,128)(2,1)})) %all-reduce.18.cloned.1.call-update) | async-done | bytes 65552 | tf_op jit(solution)/shard_map/psum | solution.py:114
  347.5 16.4 %all-reduce.10.cloned.1.call-done = bf16[512,1024]{1,0:T(8,128)(2,1)} async-done(((bf16[512,1024]{1,0:T(8,128)(2,1)}), bf16[512,1024]{1,0:T(8,128)(2,1)}) %all-reduce.10.cloned.1.call-update) | async-done | bytes 1048592 | tf_op jit(solution)/shard_map/psum | solution.py:113
  363.9 4.1 fusion.9
  368.0 12.2 %psum.89 = f32[512]{0:T(512)S(1)} all-reduce(f32[512]{0:T(512)S(1)} %get-tuple-element.35), channel_id=1, replica_groups=mesh['dp'=4,'seq'=4,'tp'=2] {'seq'}, use_global_device_ids=true, to_apply=%region_9.0 | all-reduce | flops 512 | bytes 4096 | tf_op jit(solution)/shard_map/psum | solution.py:71
  383.4 11.4 %convolution_convert_fusion = bf16[512,5120]{1,0:T(8,128)(2,1)} fusion(bf16[512,1024]{1,0:T(8,128)(2,1)S(1)} %fusion.12, bf16[5120,1024]{1,0:T(8,128)(2,1)} %param.27), kind=kOutput, calls=%fused_computation.10 | convolution fusion | flops 5371330560 | bytes 16777216 | tf_op jit(solution)/shard_map/dot_general | solution.py:11
  394.8 7.1 %multiply_convert_fusion.2 = bf16[20,512,128]{1,2,0:T(8,128)(2,1)} fusion(bf16[512,20,128]{0,2,1:T(8,128)(2,1)S(1)} %bitcast.59, bf16[20,512,512]{1,2,0:T(8,128)(2,1)} %multiply_convert_fusion), kind=kOutput, calls=%fused_computation.12 | convolution fusion | flops 1344798720 | bytes 15728640 | tf_op jit(solution)/shard_map/hij,jhd->ihd/dot_general | solution.py:46
  402.0 4.4 copy.43
  406.3 7.6 %all-reduce.16.cloned.1.call-done = (bf16[1024,32]{0,1:T(8,128)(2,1)}, bf16[32,2560]{1,0:T(8,128)(2,1)}, bf16[1024,32]{0,1:T(8,128)(2,1)}, bf16[32,2560]{1,0:T(8,128)(2,1)}) async-done(((bf16[1024,32]{0,1:T(8,128)(2,1)}, bf16[32,2560]{1,0:T(8,128)(2,1)}, bf16[1024,32]{0,1:T(8,128)(2,1)}, bf16[32,2560]{1,0:T(8,128)(2,1)}), (bf16[1024,32]{0,1:T(8,128)(2,1)}, bf16[32,2560]{1,0:T(8,128)(2,1)}, ...) | async-done | bytes 458768 | tf_op jit(solution)/shard_map/psum | solution.py:135
  417.4 93.1 %reduce-scatter.2.cloned.1.call-done = bf16[128,5120]{1,0:T(8,128)(2,1)} async-done(((bf16[512,5120]{1,0:T(8,128)(2,1)}), bf16[128,5120]{1,0:T(8,128)(2,1)}) %reduce-scatter.2.cloned.1.call-update) | async-done | bytes 1310736 | tf_op jit(solution)/shard_map/reduce_scatter | solution.py:140
  (45 shorter events, 25.4 us)
Async XLA Ops:
  7.2 275.2 %copy-start = (bf16[32,2560]{1,0:T(8,128)(2,1)S(1)}, bf16[32,2560]{1,0:T(8,128)(2,1)}, u32[]{:S(2)}) copy-start(bf16[32,2560]{1,0:T(8,128)(2,1)} %param.26) | copy-start | bytes 491524
  7.2 275.2 %all-reduce.14.cloned.1.call-start = ((), (), s32[]{:S(2)}) async-start(), calls=%async_computation.4 | async-start | bytes 10485760 | tf_op jit(solution)/shard_map/psum | solution.py:100
  90.5 0.8 copy-start.7
  90.5 0.8 copy-start.9
  90.5 3.1 copy-start.8
  90.6 229.4 %all-reduce.12.cloned.1.call-start = ((), (), s32[]{:S(2)}) async-start(), calls=%async_computation.3 | async-start | bytes 524288 | tf_op jit(solution)/shard_map/psum | solution.py:102
  96.0 244.5 %all-reduce.18.cloned.1.call-start = ((), (), s32[]{:S(2)}) async-start(), calls=%async_computation.6 | async-start | bytes 131072 | tf_op jit(solution)/shard_map/psum | solution.py:114
  282.4 3.1 copy-start.1
  285.5 5.1 copy-start.2
  290.5 6.4 %copy-start.4 = (bf16[32,2560]{1,0:T(8,128)(2,1)S(1)}, bf16[32,2560]{1,0:T(8,128)(2,1)}, u32[]{:S(2)}) copy-start(bf16[32,2560]{1,0:T(8,128)(2,1)} %param.24) | copy-start | bytes 491524
  299.9 64.0 %all-reduce.10.cloned.1.call-start = ((), (), s32[]{:S(2)}) async-start(), calls=%async_computation.1 | async-start | bytes 2097152 | tf_op jit(solution)/shard_map/psum | solution.py:113
  320.0 3.5 copy-start.6
  323.4 90.5 %all-reduce.16.cloned.1.call-start = ((), (), s32[]{:S(2)}) async-start(), calls=%async_computation.5 | async-start | bytes 917504 | tf_op jit(solution)/shard_map/psum | solution.py:135
  340.5 23.4 %copy-start.5 = (bf16[512,32]{0,1:T(8,128)(2,1)S(1)}, bf16[512,32]{0,1:T(8,128)(2,1)}, u32[]{:S(2)}) copy-start(bf16[512,32]{0,1:T(8,128)(2,1)} %get-tuple-element.30) | copy-start | bytes 98308
  347.4 32.8 %copy-start.10 = (f32[1,512]{1,0:T(1,128)S(1)}, f32[1,512]{1,0:T(1,128)}, u32[]{:S(2)}) copy-start(f32[1,512]{1,0:T(1,128)} %param.19) | copy-start | bytes 6148
  347.5 163.0 %reduce-scatter.2.cloned.1.call-start = ((), (), s32[]{:S(2)}) async-start(), calls=%async_computation.2 | async-start | bytes 6553600 | tf_op jit(solution)/shard_map/reduce_scatter | solution.py:140
  382.4 1.0 copy-start.3
Sparse Core Ops, SparseCore 0:
  90.7 191.6 all-reduce.13
  285.3 34.6 all-reduce.11
  322.9 17.5 all-reduce.17
  343.2 20.6 all-reduce.9
  367.6 46.3 all-reduce.15
  416.7 93.7 reduce-scatter.1
where the time goes:
time: 518 us; the launch traced here: 517 us
  waiting for transfers between devices  337 us (65%)
  matrix products  107 us (21%)
  other arithmetic  24.4 us (5%)
  local copies, waits for them, and re-layouts  22.3 us (4%)
  between operations  14.2 us (3%)
  blocking collectives  12.2 us (2%)
    psum x1, waiting for transfers between devices, shards(): lax.psum(grad_key.astype(jnp.bfloat16), 'seq').astype(jnp.float32)  186 us
    reduce_scatter x1, waiting for transfers between devices, shards(): lax.psum_scatter(contract_last(grad_text, out_weight).astype(jnp.bfloat16...  93.1 us
    dot_general x7, matrix products, contract_last(): lax.dot_general(left_side, right_side, (((1,), (1,)), ((), ())), preferre...  35.5 us
    unnamed x27, local copies, waits for them, and re-layouts  22.3 us
    psum x1, waiting for transfers between devices, shards(): lax.psum(key_part.astype(jnp.bfloat16), 'seq').astype(jnp.float32)  20 us
    convert_element_type x1, other arithmetic, attention_grads(): grad_low = grad_scores.astype(jnp.bfloat16)  18.7 us
    psum x1, waiting for transfers between devices, shards(): lax.psum(context_part.astype(jnp.bfloat16), 'tp').astype(jnp.float32)  16.4 us
    dot_general x1, matrix products, attention_grads(): jnp.einsum('ihd,jhd->hij', grad_heads, value_heads, preferred_element_typ...  15.6 us
  transfers between devices with their start and end apart: 6, of which 6 were waited for; matrix products, arithmetic and copies ran while one was open for 13% of the time, Pallas kernels for 0%

commit v1 on v0

--- a/solution.py
+++ b/solution.py
@@ -97,7 +97,7 @@
     key_part = jnp.dot(context, key_down, preferred_element_type=jnp.float32)
     value_part = jnp.dot(context, value_down, preferred_element_type=jnp.float32)
     key_sum, value_sum, key_lowsum, value_lowsum = (
-        lax.psum(grad_key.astype(jnp.bfloat16), "seq").astype(jnp.float32),
+        jnp.sum(lax.all_gather(grad_key.astype(jnp.bfloat16), "seq"), axis=0).astype(jnp.float32),
         lax.psum(grad_value.astype(jnp.bfloat16), "seq").astype(jnp.float32),
         lax.psum(key_part.astype(jnp.bfloat16), "seq").astype(jnp.float32),
         lax.psum(value_part.astype(jnp.bfloat16), "seq").astype(jnp.float32),

time: 518 us -> 581 us (1.12)
  waiting for transfers between devices: 337 us -> 394 us
  matrix products: 107 us -> 98.9 us
  local copies, waits for them, and re-layouts: 22.3 us -> 29.6 us
    all_gather x0 -> x1, waiting for transfers between devices: none -> 183 us  [shards(): lax.all_gather(grad_key.astype(jnp.bfloat16), 'seq')]
    psum x1, waiting for transfers between devices: 186 us -> 52.2 us  [shards(): lax.psum(grad_value.astype(jnp.bfloat16), 'seq').astype(jnp.float32)]
    psum x1, waiting for transfers between devices: 20 us -> 33.3 us  [shards(): lax.psum(key_part.astype(jnp.bfloat16), 'seq').astype(jnp.float32)]
    unnamed x0 -> x1, other arithmetic: none -> 7.3 us
    psum x1, waiting for transfers between devices: 13.7 us -> 6.72 us  [shards(): lax.psum(key_project.astype(jnp.bfloat16), 'tp').astype(jnp.float32)]
    unnamed x27 -> x37, local copies, waits for them, and re-layouts: 22.3 us -> 25.2 us
  transfers between devices with their start and end apart: 6 -> 7, of which waited for: 6 -> 7; matrix products, arithmetic and copies ran while one was open for 13% -> 18% of each run, Pallas kernels for 0% -> 0%
where the time goes in v1:
time: 581 us; the launch traced here: 580 us
  waiting for transfers between devices  394 us (68%)
  matrix products  98.9 us (17%)
  other arithmetic  30.2 us (5%)
  local copies, waits for them, and re-layouts  29.6 us (5%)
  between operations  14.2 us (2%)
  blocking collectives  12 us (2%)
    all_gather x1, waiting for transfers between devices, shards(): lax.all_gather(grad_key.astype(jnp.bfloat16), 'seq')  183 us
    reduce_scatter x1, waiting for transfers between devices, shards(): lax.psum_scatter(contract_last(grad_text, out_weight).astype(jnp.bfloat16...  93.2 us
    psum x1, waiting for transfers between devices, shards(): lax.psum(grad_value.astype(jnp.bfloat16), 'seq').astype(jnp.float32)  52.2 us
    dot_general x7, matrix products, contract_last(): lax.dot_general(left_side, right_side, (((1,), (1,)), ((), ())), preferre...  35.5 us
    psum x1, waiting for transfers between devices, shards(): lax.psum(key_part.astype(jnp.bfloat16), 'seq').astype(jnp.float32)  33.3 us
    unnamed x37, local copies, waits for them, and re-layouts  25.2 us
    convert_element_type x1, other arithmetic, attention_grads(): grad_low = grad_scores.astype(jnp.bfloat16)  19 us
    psum x1, waiting for transfers between devices, shards(): lax.psum(context_part.astype(jnp.bfloat16), 'tp').astype(jnp.float32)  16.4 us
  transfers between devices with their start and end apart: 7, of which 7 were waited for; matrix products, arithmetic and copies ran while one was open for 18% of the time, Pallas kernels for 0%

profile of v1, /device:TPU:0, one launch (start us, length us, event | category | flops | bytes accessed | tf_op | source)
XLA Modules:
  0.0 579.9 jit_solution(11581285753747719634)
XLA Ops:
  7.2 4.5 copy.44
  14.7 5.0 copy.48
  19.7 12.1 %fusion.22 = (f32[20,512]{1,0:T(8,128)S(1)}, f32[20,512,512]{1,2,0:T(8,128)}) fusion(bf16[512,20,128]{0,2,1:T(8,128)(2,1)} %bitcast.62, bf16[512,20,128]{0,2,1:T(8,128)(2,1)S(1)} %bitcast.58), kind=kOutput, calls=%fused_computation.39 | convolution fusion | flops 1357906432 | bytes 26255360 | tf_op jit(solution)/shard_map/sub | solution.py:35
  31.8 10.9 %fusion.14 = bf16[20,512,128]{1,2,0:T(8,128)(2,1)} fusion(bf16[512,20,128]{0,2,1:T(8,128)(2,1)} %bitcast.64, f32[20,512,512]{1,2,0:T(8,128)} %get-tuple-element.37, f32[20,512]{1,0:T(8,128)S(1)} %get-tuple-element.36), kind=kOutput, calls=%fused_computation.26 | convolution fusion | flops 1353973760 | bytes 26255360 | tf_op jit(solution)/shard_map/hij,ihd->jhd/dot_general | solution.py:52
  46.3 4.5 copy.49
  50.8 14.2 %multiply_reduce_fusion = (f32[20,512]{1,0:T(8,128)S(1)}, f32[20,512,512]{1,2,0:T(8,128)}) fusion(f32[20,512,512]{1,2,0:T(8,128)} %get-tuple-element.37, f32[20,512]{1,0:T(8,128)S(1)} %get-tuple-element.36, bf16[512,20,128]{0,2,1:T(8,128)(2,1)S(1)} %bitcast.65, bf16[512,20,128]{0,2,1:T(8,128)(2,1)} %bitcast.66), kind=kOutput, calls=%fused_computation.2 | convolution fusion | flops 1357895680 | bytes 47267840 | tf_op jit(solution)/shard_map/ihd,jhd->hij/dot_general | solution.py:38
  65.0 19.0 %multiply_convert_fusion = bf16[20,512,512]{1,2,0:T(8,128)(2,1)} fusion(f32[20,512,512]{1,2,0:T(8,128)} %get-tuple-element.39, f32[20,512]{1,0:T(8,128)S(1)} %get-tuple-element.38, f32[20,512,512]{1,2,0:T(8,128)} %get-tuple-element.37, f32[20,512]{1,0:T(8,128)S(1)} %get-tuple-element.36), kind=kLoop, calls=%fused_computation.1 | loop fusion | flops 20971520 | bytes 52510720 | tf_op jit(solution)/shard_map/convert_element_type | solution.py:44
  84.0 9.0 %multiply_convert_fusion.1 = bf16[20,512,128]{1,2,0:T(8,128)(2,1)} fusion(bf16[20,512,512]{1,2,0:T(8,128)(2,1)} %multiply_convert_fusion, bf16[512,20,128]{0,2,1:T(8,128)(2,1)S(1)} %bitcast.63), kind=kOutput, calls=%fused_computation.11 | convolution fusion | flops 1344798720 | bytes 15728640 | tf_op jit(solution)/shard_map/hij,ihd->jhd/dot_general | solution.py:49
  93.0 4.4 copy.54
  97.5 52.2 %all-reduce.9.cloned.1.call-done = bf16[512,2560]{0,1:T(8,128)(2,1)} async-done(((bf16[512,2560]{0,1:T(8,128)(2,1)}), bf16[512,2560]{0,1:T(8,128)(2,1)}) %all-reduce.9.cloned.1.call-update) | async-done | bytes 2621456 | tf_op jit(solution)/shard_map/psum | solution.py:101
  149.7 3.1 convolution_convert_fusion.5
  152.8 33.3 %all-reduce.13.cloned.1.call-done = (bf16[512,32]{0,1:T(8,128)(2,1)}, bf16[512,32]{0,1:T(8,128)(2,1)}) async-done(((bf16[512,32]{0,1:T(8,128)(2,1)}, bf16[512,32]{0,1:T(8,128)(2,1)}), (bf16[512,32]{0,1:T(8,128)(2,1)}, bf16[512,32]{0,1:T(8,128)(2,1)})) %all-reduce.13.cloned.1.call-update) | async-done | bytes 65552 | tf_op jit(solution)/shard_map/psum | solution.py:102
  188.3 182.9 %all-gather.2.cloned.1.call-done = bf16[4,512,2560]{2,1,0:T(8,128)(2,1)} async-done(((bf16[1,512,2560]{2,1,0:T(8,128)(2,1)}), bf16[4,512,2560]{2,1,0:T(8,128)(2,1)}) %all-gather.2.cloned.1.call-update) | async-done | bytes 10485776 | tf_op jit(solution)/shard_map/all_gather | solution.py:100
  371.3 7.3 %reduce_sum.41 = bf16[512,2560]{1,0:T(8,128)(2,1)S(1)} reduce(bf16[4,512,2560]{2,1,0:T(8,128)(2,1)} %all-gather.2.cloned.1.call-done, bf16[]{:T(256)} %constant.16.clone.1), dimensions={0}, to_apply=%region_3.0 | reduce | flops 3932160 | bytes 13107202
  380.1 6.7 %fusion.23 = f32[512,1024]{1,0:T(8,128)} fusion(bf16[512,2560]{1,0:T(8,128)(2,1)S(1)} %reduce_sum.41, bf16[1024,2560]{1,0:T(8,128)(2,1)} %param.21), kind=kOutput, calls=%fused_computation.40 | convolution fusion | flops 2684354560 | bytes 9961472 | tf_op jit(solution)/shard_map/dot_general | solution.py:11
  387.1 7.8 %add_convert_fusion = bf16[512,1024]{1,0:T(8,128)(2,1)} fusion(f32[512,1024]{1,0:T(8,128)} %fusion.23, bf16[512,2560]{0,1:T(8,128)(2,1)} %all-reduce.9.cloned.1.call-done, bf16[1024,2560]{1,0:T(8,128)(2,1)} %param.22), kind=kOutput, calls=%fused_computation.25 | convolution fusion | flops 2685403136 | bytes 11010048 | tf_op jit(solution)/shard_map/dot_general | solution.py:11
  396.2 6.7 %all-reduce.17.cloned.1.call-done = (bf16[512,32]{0,1:T(8,128)(2,1)}, bf16[512,32]{0,1:T(8,128)(2,1)}) async-done(((bf16[512,32]{0,1:T(8,128)(2,1)}, bf16[512,32]{0,1:T(8,128)(2,1)}), (bf16[512,32]{0,1:T(8,128)(2,1)}, bf16[512,32]{0,1:T(8,128)(2,1)})) %all-reduce.17.cloned.1.call-update) | async-done | bytes 65552 | tf_op jit(solution)/shard_map/psum | solution.py:114
  410.0 16.4 %all-reduce.11.cloned.1.call-done = bf16[512,1024]{1,0:T(8,128)(2,1)} async-done(((bf16[512,1024]{1,0:T(8,128)(2,1)}), bf16[512,1024]{1,0:T(8,128)(2,1)}) %all-reduce.11.cloned.1.call-update) | async-done | bytes 1048592 | tf_op jit(solution)/shard_map/psum | solution.py:113
  428.9 12.0 %psum.81 = f32[512]{0:T(512)S(1)} all-reduce(f32[512]{0:T(512)S(1)} %get-tuple-element.40), channel_id=1, replica_groups=mesh['dp'=4,'seq'=4,'tp'=2] {'seq'}, use_global_device_ids=true, to_apply=%region_9.0 | all-reduce | flops 512 | bytes 4096 | tf_op jit(solution)/shard_map/psum | solution.py:71
  442.3 11.3 %convolution_convert_fusion = bf16[512,5120]{1,0:T(8,128)(2,1)} fusion(bf16[512,1024]{1,0:T(8,128)(2,1)S(1)} %fusion.12, bf16[5120,1024]{1,0:T(8,128)(2,1)} %param.27), kind=kOutput, calls=%fused_computation.10 | convolution fusion | flops 5371330560 | bytes 16777216 | tf_op jit(solution)/shard_map/dot_general | solution.py:11
  455.4 7.1 %multiply_convert_fusion.2 = bf16[20,512,128]{1,2,0:T(8,128)(2,1)} fusion(bf16[512,20,128]{0,2,1:T(8,128)(2,1)S(1)} %bitcast.59, bf16[20,512,512]{1,2,0:T(8,128)(2,1)} %multiply_convert_fusion), kind=kOutput, calls=%fused_computation.12 | convolution fusion | flops 1344798720 | bytes 15728640 | tf_op jit(solution)/shard_map/hij,jhd->ihd/dot_general | solution.py:46
  462.5 4.4 copy.57
  466.8 9.6 %all-reduce.15.cloned.1.call-done = (bf16[1024,32]{0,1:T(8,128)(2,1)}, bf16[32,2560]{1,0:T(8,128)(2,1)}, bf16[1024,32]{0,1:T(8,128)(2,1)}, bf16[32,2560]{1,0:T(8,128)(2,1)}) async-done(((bf16[1024,32]{0,1:T(8,128)(2,1)}, bf16[32,2560]{1,0:T(8,128)(2,1)}, bf16[1024,32]{0,1:T(8,128)(2,1)}, bf16[32,2560]{1,0:T(8,128)(2,1)}), (bf16[1024,32]{0,1:T(8,128)(2,1)}, bf16[32,2560]{1,0:T(8,128)(2,1)}, ...) | async-done | bytes 458768 | tf_op jit(solution)/shard_map/psum | solution.py:135
  479.9 93.2 %reduce-scatter.2.cloned.1.call-done = bf16[128,5120]{1,0:T(8,128)(2,1)} async-done(((bf16[512,5120]{1,0:T(8,128)(2,1)}), bf16[128,5120]{1,0:T(8,128)(2,1)}) %reduce-scatter.2.cloned.1.call-update) | async-done | bytes 1310736 | tf_op jit(solution)/shard_map/reduce_scatter | solution.py:140
  (60 shorter events, 28.1 us)
Async XLA Ops:
  7.2 142.5 %copy-start = (bf16[32,2560]{1,0:T(8,128)(2,1)S(1)}, bf16[32,2560]{1,0:T(8,128)(2,1)}, u32[]{:S(2)}) copy-start(bf16[32,2560]{1,0:T(8,128)(2,1)} %param.26) | copy-start | bytes 491524
  7.2 142.5 %all-reduce.9.cloned.1.call-start = ((), (), s32[]{:S(2)}) async-start(), calls=%async_computation.2 | async-start | bytes 5242880 | tf_op jit(solution)/shard_map/psum | solution.py:101
  14.7 5.0 copy-start.1
  42.7 1.2 copy-start.3
  42.7 1.2 copy-start.11
  42.7 1.2 copy-start.13
  42.7 2.3 copy-start.12
  42.8 143.3 %all-reduce.13.cloned.1.call-start = ((), (), s32[]{:S(2)}) async-start(), calls=%async_computation.5 | async-start | bytes 131072 | tf_op jit(solution)/shard_map/psum | solution.py:102
  46.0 4.8 copy-start.7
  46.1 325.2 %all-gather.2.cloned.1.call-start = ((), (), s32[]{:S(2)}) async-start(), calls=%async_computation.1 | async-start | bytes 13107200 | tf_op jit(solution)/shard_map/all_gather | solution.py:100
  65.0 19.0 %copy-start.6 = (bf16[1,512,2560]{1,2,0:T(8,128)(2,1)S(1)}, bf16[1,512,2560]{1,2,0:T(8,128)(2,1)}, u32[]{:S(2)}) copy-start(bf16[1,512,2560]{1,2,0:T(8,128)(2,1)} %copy.44) | copy-start | bytes 7864324
  97.5 305.5 %all-reduce.17.cloned.1.call-start = ((), (), s32[]{:S(2)}) async-start(), calls=%async_computation.7 | async-start | bytes 131072 | tf_op jit(solution)/shard_map/psum | solution.py:114
  149.7 36.3 %copy-start.5 = (bf16[512,2560]{0,1:T(8,128)(2,1)S(1)}, bf16[512,2560]{0,1:T(8,128)(2,1)}, u32[]{:S(2)}) copy-start(bf16[512,2560]{0,1:T(8,128)(2,1)} %all-reduce.9.cloned.1.call-done) | copy-start | bytes 7864324
  188.3 190.2 %copy-start.9 = (bf16[32,2560]{1,0:T(8,128)(2,1)S(1)}, bf16[32,2560]{1,0:T(8,128)(2,1)}, u32[]{:S(2)}) copy-start(bf16[32,2560]{1,0:T(8,128)(2,1)} %param.24) | copy-start | bytes 491524
  386.8 8.2 %copy-start.14 = (bf16[512,32]{0,1:T(8,128)(2,1)S(1)}, bf16[512,32]{0,1:T(8,128)(2,1)}, u32[]{:S(2)}) copy-start(bf16[512,32]{0,1:T(8,128)(2,1)} %get-tuple-element.28) | copy-start | bytes 98308
  386.8 39.5 %all-reduce.11.cloned.1.call-start = ((), (), s32[]{:S(2)}) async-start(), calls=%async_computation.3 | async-start | bytes 2097152 | tf_op jit(solution)/shard_map/psum | solution.py:113
  394.9 81.5 %all-reduce.15.cloned.1.call-start = ((), (), s32[]{:S(2)}) async-start(), calls=%async_computation.6 | async-start | bytes 917504 | tf_op jit(solution)/shard_map/psum | solution.py:135
  396.2 30.1 %copy-start.4 = (bf16[1,512,1024]{2,1,0:T(8,128)(2,1)S(1)}, bf16[1,512,1024]{2,1,0:T(8,128)(2,1)}, u32[]{:S(2)}) copy-start(bf16[1,512,1024]{2,1,0:T(8,128)(2,1)} %param.18) | copy-start | bytes 3145732
  402.9 23.4 %copy-start.10 = (bf16[512,32]{0,1:T(8,128)(2,1)S(1)}, bf16[512,32]{0,1:T(8,128)(2,1)}, u32[]{:S(2)}) copy-start(bf16[512,32]{0,1:T(8,128)(2,1)} %get-tuple-element.35) | copy-start | bytes 98308
  409.9 31.0 %copy-start.15 = (f32[1,512]{1,0:T(1,128)S(1)}, f32[1,512]{1,0:T(1,128)}, u32[]{:S(2)}) copy-start(f32[1,512]{1,0:T(1,128)} %param.19) | copy-start | bytes 6148
  409.9 163.1 %reduce-scatter.2.cloned.1.call-start = ((), (), s32[]{:S(2)}) async-start(), calls=%async_computation.4 | async-start | bytes 6553600 | tf_op jit(solution)/shard_map/reduce_scatter | solution.py:140
  441.3 1.0 copy-start.8
  453.6 1.7 copy-start.2
Sparse Core Ops, SparseCore 0:
  42.9 106.7 all-reduce.8
  152.6 33.3 all-reduce.12
  187.6 183.6 all-gather.1
  386.9 15.9 all-reduce.16
  405.7 20.6 all-reduce.10
  430.0 46.3 all-reduce.14
  479.3 93.7 reduce-scatter.1
